TPU v7x, 32 devices: a whole 2x2x4 slice. The times are simulated.
32 devices in a mesh: dp: 16 (over z, y, x), tensor: 2 (over core).
Axes of the slice: x: 2, y: 2, z: 4, core: 2. Of those that a mesh axis runs over, the one named last changes fastest.
Arguments:
- current: float32 [32, 4096], P('dp'), may hold values from -6 to 6
- noise_draw: float32 [32, 4096], P('dp'), may hold values from -6 to 6
- labels: bfloat16 [32, 1152], P('dp'), may hold values from -6 to 6
- time_now: float32 [32], P('dp'), may hold values from 0.4 to 1
- step_size: float32 [32], P('dp'), may hold values from 0.005 to 0.02
- accept: int32 [32], P('dp'), may hold values 0 or 1
- patch_weight: bfloat16 [16, 1152], replicated, may hold values from -1.5 to 1.5
- time_in: bfloat16 [256, 1152], replicated, may hold values from -0.375 to 0.375
- time_out: bfloat16 [1152, 1152], replicated, may hold values from -0.1875 to 0.1875
- qkv_weight: bfloat16 [1, 1152, 3, 1152], P(None, None, None, 'tensor'), may hold values from -1 to 1
- out_weight: bfloat16 [1, 1152, 1152], P(None, None, 'tensor'), may hold values from -0.1875 to 0.1875
- ada_weight: bfloat16 [1, 1152, 3456], P(None, 'dp', 'tensor'), may hold values from -0.1875 to 0.1875
- final_ada: bfloat16 [1152, 2304], P('dp', 'tensor'), may hold values from -0.1875 to 0.1875
- final_proj: bfloat16 [1152, 16], replicated, may hold values from -0.1875 to 0.1875
Outputs:
- next_state: float32 [32, 4096], P('dp')
- error_norm: float32 [32], P('dp')
All inputs are finite; a program needn't handle non-finite values. No bound on the sum of `accept` on one device may be relied on, other than what follows from the above.
Results may differ from a plain program's by a relative error of at most 0.015.
Values may be sent and summed in bfloat16 or wider, within the bound.
No kernel may reach another device: no remote copies, remote signals or barrier semaphores. Data moves between devices by JAX's collectives and lax.ppermute only.
A program may use at most 128 MiB of HBM per device.

v0:
```python
import math
import jax
import jax.numpy as jnp
from jax import lax
from jax.sharding import PartitionSpec as P

D = 1152
PATCH_VALS = 16
HEAD_DIM = 72
beta_low = 0.1
beta_high = 20.0
tol_abs = 0.0078
tol_rel = 0.05
norm_eps = 1e-06


def beta_at(moments):
    return beta_low + (beta_high - beta_low) * moments


def sigma_at(moments):
    integral = beta_low * moments + 0.5 * (beta_high - beta_low) * moments * moments
    return jnp.sqrt(1.0 - jnp.exp(-integral))


def time_features(moments, feature_count):
    half_count = feature_count // 2
    freq_index = jnp.arange(half_count, dtype=jnp.float32)
    freq_rates = jnp.exp(-math.log(10000.0) * freq_index / half_count)
    angles = 1000.0 * moments[:, None] * freq_rates[None, :]
    return jnp.concatenate([jnp.cos(angles), jnp.sin(angles)], axis=1)


def position_table(positions, feature_count):
    half_count = feature_count // 2
    freq_index = jnp.arange(half_count, dtype=jnp.float32)
    freq_rates = jnp.exp(-math.log(10000.0) * freq_index / half_count)
    angles = positions.astype(jnp.float32)[:, None] * freq_rates[None, :]
    return jnp.concatenate([jnp.sin(angles), jnp.cos(angles)], axis=1)


def condition(moments, labels, time_in, time_out):
    features = time_features(moments, time_in.shape[0]).astype(jnp.bfloat16)
    hidden = jax.nn.silu(jnp.dot(features, time_in, preferred_element_type=jnp.float32)).astype(
        jnp.bfloat16
    )
    joined = labels.astype(jnp.float32) + jnp.dot(
        hidden, time_out, preferred_element_type=jnp.float32
    )
    return jax.nn.silu(joined).astype(jnp.bfloat16)


def layer_norm(values):
    average = jnp.mean(values, axis=-1, keepdims=True)
    centred = values - average
    spread_sq = jnp.mean(centred * centred, axis=-1, keepdims=True)
    return centred * lax.rsqrt(spread_sq + norm_eps)


def modulate(values, shift_vec, scale_vec):
    return (layer_norm(values) * (1.0 + scale_vec[:, None]) + shift_vec[:, None]).astype(
        jnp.bfloat16
    )


def drift(values, moments, noise_guess):
    beta_rate = beta_at(moments)[:, None]
    return 0.5 * beta_rate * values - beta_rate * noise_guess / sigma_at(moments)[:, None]


def attend(projected, head_dim):
    lat_count, token_count, _, feature_width = projected.shape
    head_count = feature_width // head_dim
    shaped = projected.reshape(lat_count, token_count, 3, head_count, head_dim)
    scores = jnp.einsum(
        "lqhe,lkhe->lhqk", shaped[:, :, 0], shaped[:, :, 1], preferred_element_type=jnp.float32
    ) * head_dim ** (-0.5)
    attn_probs = jax.nn.softmax(scores, axis=-1).astype(jnp.bfloat16)
    mixture = jnp.einsum(
        "lhqk,lkhe->lqhe", attn_probs, shaped[:, :, 2], preferred_element_type=jnp.float32
    )
    return mixture.astype(jnp.bfloat16).reshape(lat_count, token_count, feature_width)


def shards(
    current,
    noise_draw,
    labels,
    time_now,
    step_size,
    accept,
    patch_weight,
    time_in,
    time_out,
    qkv_weight,
    out_weight,
    ada_weight,
    final_ada,
    final_proj,
):
    lat_count = current.shape[0]
    tok_count = current.shape[1] // PATCH_VALS
    layer_total = ada_weight.shape[0]
    layer_cols = ada_weight.shape[2]
    final_cols = final_ada.shape[1]
    tensor_size = lax.axis_size("tensor")
    later_time = time_now - step_size
    moments = jnp.concatenate([time_now, later_time])
    cond_act = condition(moments, jnp.concatenate([labels, labels], axis=0), time_in, time_out)
    own_rows = ada_weight.shape[1]
    packed = jnp.concatenate(
        [ada_weight.transpose(1, 0, 2).reshape(own_rows, layer_total * layer_cols), final_ada],
        axis=1,
    )
    row_total = cond_act.shape[0]
    packed_width = packed.shape[1]
    mod_local = jnp.dot(
        cond_act,
        lax.all_gather(packed, "dp", axis=0, tiled=True),
        preferred_element_type=jnp.float32,
    )
    gathered = lax.all_gather(mod_local.astype(jnp.bfloat16), "tensor", axis=1, tiled=True).astype(
        mod_local.dtype
    )
    arranged = gathered.reshape(row_total, tensor_size, packed_width)
    layer_mods = arranged[:, :, : layer_total * layer_cols].reshape(
        row_total, tensor_size, layer_total, layer_cols
    )
    layer_mods = layer_mods.transpose(0, 2, 1, 3).reshape(
        row_total, layer_total, tensor_size * layer_cols
    )
    final_mods = arranged[:, :, layer_total * layer_cols :].reshape(
        row_total, tensor_size * final_cols
    )
    positions = position_table(jnp.arange(tok_count, dtype=jnp.int32), D)

    def evaluate(latents, mod_rows, final_rows):
        tokens = latents.reshape(lat_count, tok_count, PATCH_VALS).astype(jnp.bfloat16)
        stream = (
            jnp.einsum("ltc,cd->ltd", tokens, patch_weight, preferred_element_type=jnp.float32)
            + positions[None]
        )
        shift_attn, scale_attn, gate_attn = jnp.split(mod_rows[:, 0], 3, axis=1)
        attn_in = modulate(stream, shift_attn, scale_attn)
        projected = jnp.einsum(
            "ltd,dck->ltck", attn_in, qkv_weight[0], preferred_element_type=jnp.float32
        ).astype(jnp.bfloat16)
        attended = attend(projected, HEAD_DIM)
        partial_value = jnp.einsum(
            "ltk,dk->ltd", attended, out_weight[0], preferred_element_type=jnp.float32
        )
        attn_sum = lax.psum(partial_value.astype(jnp.bfloat16), "tensor").astype(jnp.float32)
        stream = stream + gate_attn[:, None] * attn_sum
        shift_final, scale_final = jnp.split(final_rows, 2, axis=1)
        final_in = modulate(stream, shift_final, scale_final)
        guessed = jnp.einsum(
            "ltd,dc->ltc", final_in, final_proj, preferred_element_type=jnp.float32
        )
        return guessed.reshape(lat_count, tok_count * PATCH_VALS)

    noise_now = evaluate(current, layer_mods[:lat_count], final_mods[:lat_count])
    drift_now = drift(current, time_now, noise_now)
    spread = jnp.sqrt(step_size * beta_at(time_now))[:, None] * noise_draw
    euler_state = current + step_size[:, None] * drift_now + spread
    noise_later = evaluate(euler_state, layer_mods[lat_count:], final_mods[lat_count:])
    drift_later = drift(euler_state, later_time, noise_later)
    heun_state = current + 0.5 * step_size[:, None] * (drift_now + drift_later) + spread
    scale_ref = jnp.maximum(tol_abs, tol_rel * jnp.maximum(jnp.abs(heun_state), jnp.abs(current)))
    scaled_gap = (euler_state - heun_state) / scale_ref
    error_norm = jnp.sqrt(jnp.sum(scaled_gap * scaled_gap, axis=1) / current.shape[1])
    next_state = jnp.where(accept[:, None] == 1, heun_state, current)
    return (next_state, error_norm)


def solution(mesh):
    in_specs = (
        P("dp", None),
        P("dp", None),
        P("dp", None),
        P("dp"),
        P("dp"),
        P("dp"),
        P(),
        P(),
        P(),
        P(None, None, None, "tensor"),
        P(None, None, "tensor"),
        P(None, "dp", "tensor"),
        P("dp", "tensor"),
        P(),
    )
    out_specs = (P("dp", None), P("dp"))
    return jax.shard_map(shards, mesh=mesh, in_specs=in_specs, out_specs=out_specs, check_vma=False)
```

profile of v0, /device:TPU:0, one launch (start us, length us, event | category | flops | bytes accessed | tf_op | source)
XLA Modules:
  0.0 200.8 jit_solution(1456404934504818593)
XLA Ops:
  7.2 2.1 %pad_maximum_fusion.1 = bf16[72,2880]{1,0:T(8,128)(2,1)} fusion(bf16[72,1152]{1,0:T(8,128)(2,1)} %param.26, bf16[72,1728]{1,0:T(8,128)(2,1)} %bitcast.104), kind=kLoop, calls=%fused_computation.66 | loop fusion | flops 829440 | bytes 829440 | tf_op jit(solution)/shard_map/concatenate | solution.py:111
  9.4 0.8 convert_element_type.83
  10.3 0.7 broadcast_multiply_fusion.4
  11.0 0.7 maximum_multiply_fusion
  11.8 2.4 %multiply_sine_fusion = (f32[256,576]{1,0:T(8,128)S(1)}, f32[256,576]{1,0:T(8,128)S(1)}) fusion(f32[576]{0:T(1024)S(1)} %multiply_exponential_fusion, f32[256]{0:T(256)S(1)} %iota_convert_fusion), kind=kLoop, calls=%fused_computation.55 | loop fusion | flops 147456 | bytes 1182976 | tf_op jit(solution)/shard_map/sin | solution.py:39
  14.4 1.0 copy-done.5
  15.4 0.5 fusion.78
  15.9 1.4 copy-done.1
  18.1 93.2 %all-gather.3.cloned.1.call-done = bf16[1152,2880]{1,0:T(8,128)(2,1)} async-done(((bf16[72,2880]{1,0:T(8,128)(2,1)}), bf16[1152,2880]{1,0:T(8,128)(2,1)}) %all-gather.3.cloned.1.call-update) | async-done | bytes 6635536 | tf_op jit(solution)/shard_map/all_gather | solution.py:119
  111.3 4.3 %fusion.8 = bf16[1,2880,4]{1,2,0:T(4,128)(2,1)S(1)} fusion(bf16[1152,2880]{1,0:T(8,128)(2,1)} %all-gather.3.cloned.1.call-done, bf16[1152,1152]{1,0:T(8,128)(2,1)S(1)} %copy-done, f32[4,1152]{1,0:T(4,128)S(1)} %fusion.62, bf16[2,1152]{1,0:T(2,128)(2,1)S(1)} %copy-done.12), kind=kOutput, calls=%fused_computation.17 | convolution fusion | flops 37239552 | bytes 9335808 | tf_op jit(solution)/shard_map/dot_general | solution.py:117
  115.6 1.8 all-gather
  118.0 5.6 %fusion.17 = bf16[2,256,3,576]{1,3,2,0:T(8,128)(2,1)S(1)} fusion(bf16[1,1152,3,576]{1,3,2,0:T(8,128)(2,1)} %param.23, f32[2,256,1152]{2,1,0:T(8,128)} %copy-done.1, f32[2,1152]{1,0:T(2,128)S(1)} %get-tuple-element.17, f32[2,1152]{1,0:T(2,128)S(1)} %get-tuple-element.18, f32[2,256]{1,0:T(2,128)S(1)} %add_rsqrt_fusion.3, ...), kind=kOutput, calls=%fused_computation.35 | convolution fusion | flops 2042265600 | bytes 8132608 | tf_op jit(solution)/shard_map/ltd,dck->ltck/dot_general | solution.py:145
  123.6 0.7 fusion.44
  124.3 3.2 %fusion.79 = (f32[2,8,256]{2,1,0:T(8,128)S(1)}, f32[2,8,256,256]{2,3,1,0:T(8,128)S(1)}) fusion(f32[2,8,256,256]{2,3,1,0:T(8,128)S(1)} %fusion.44), kind=kOutput, calls=%fused_computation.137 | output fusion | flops 4194559 | bytes 8404992 | tf_op jit(solution)/shard_map/sub | solution.py:78
  128.1 0.8 copy-done.15
  128.9 2.2 %convolution_convert_fusion.2 = bf16[2,256,1152]{2,1,0:T(8,128)(2,1)} fusion(bf16[2,256,576]{1,2,0:T(8,128)(2,1)S(1)} %bitcast.107, bf16[1,1152,576]{1,2,0:T(8,128)(2,1)S(1)} %copy-done.15), kind=kOutput, calls=%fused_computation.19 | convolution fusion | flops 680067072 | bytes 3096576 | tf_op jit(solution)/shard_map/ltk,dk->ltd/dot_general | solution.py:149
  131.5 17.9 %all-reduce.3.cloned.1.call-done = bf16[2,256,1152]{2,1,0:T(8,128)(2,1)} async-done(((bf16[2,256,1152]{2,1,0:T(8,128)(2,1)}), bf16[2,256,1152]{2,1,0:T(8,128)(2,1)}) %all-reduce.3.cloned.1.call-update) | async-done | bytes 1179664 | tf_op jit(solution)/shard_map/psum | solution.py:152
  149.4 2.5 %fusion.41 = f32[2,256]{1,0:T(2,128)S(1)} fusion(f32[2,256,1152]{2,1,0:T(8,128)} %copy-done.1, bf16[2,256,1152]{2,1,0:T(8,128)(2,1)} %all-reduce.3.cloned.1.call-done, f32[2,1152]{1,0:T(2,128)S(1)} %get-tuple-element.16), kind=kLoop, calls=%fused_computation.56 | loop fusion | flops 2358784 | bytes 3550208 | tf_op jit(solution)/shard_map/reduce_sum | solution.py:54
  152.5 0.6 multiply_reduce_fusion.4
  153.1 0.8 fusion.39
  154.4 1.9 fusion.80
  156.8 2.8 %fusion.20 = bf16[2,256,3,576]{1,3,2,0:T(8,128)(2,1)S(1)} fusion(bf16[1,1152,3,576]{1,3,2,0:T(8,128)(2,1)S(1)} %copy-done.14, f32[2,256,1152]{2,1,0:T(8,128)S(1)} %get-tuple-element.39, f32[2,1152]{1,0:T(2,128)S(1)} %get-tuple-element.14, f32[2,1152]{1,0:T(2,128)S(1)} %get-tuple-element.15, f32[2,256]{1,0:T(2,128)S(1)} %add_rsqrt_fusion.1, ...), kind=kOutput, calls=%fused_computation.36 | convolution fusion | flops 2042265600 | bytes 8132608 | tf_op jit(solution)/shard_map/ltd,dck->ltck/dot_general | solution.py:145
  159.6 0.8 fusion.43
  160.4 3.2 %fusion.81 = (f32[2,8,256]{2,1,0:T(8,128)S(1)}, f32[2,8,256,256]{2,3,1,0:T(8,128)S(1)}) fusion(f32[2,8,256,256]{2,3,1,0:T(8,128)S(1)} %fusion.43), kind=kOutput, calls=%fused_computation.139 | output fusion | flops 4194559 | bytes 8404992 | tf_op jit(solution)/shard_map/sub | solution.py:78
  164.1 0.8 copy-done.16
  164.9 2.2 %convolution_convert_fusion.1 = bf16[2,256,1152]{2,1,0:T(8,128)(2,1)} fusion(bf16[2,256,576]{1,2,0:T(8,128)(2,1)S(1)} %bitcast.108, bf16[1,1152,576]{1,2,0:T(8,128)(2,1)S(1)} %copy-done.16), kind=kOutput, calls=%fused_computation.18 | convolution fusion | flops 680067072 | bytes 3096576 | tf_op jit(solution)/shard_map/ltk,dk->ltd/dot_general | solution.py:149
  167.2 20.9 %all-reduce.5.cloned.1.call-done = bf16[2,256,1152]{2,1,0:T(8,128)(2,1)} async-done(((bf16[2,256,1152]{2,1,0:T(8,128)(2,1)}), bf16[2,256,1152]{2,1,0:T(8,128)(2,1)}) %all-reduce.5.cloned.1.call-update) | async-done | bytes 1179664 | tf_op jit(solution)/shard_map/psum | solution.py:152
  188.2 2.5 %fusion.42 = f32[2,256]{1,0:T(2,128)S(1)} fusion(f32[2,256,1152]{2,1,0:T(8,128)} %copy-done.3, bf16[2,256,1152]{2,1,0:T(8,128)(2,1)} %all-reduce.5.cloned.1.call-done, f32[2,1152]{1,0:T(2,128)S(1)} %get-tuple-element.13), kind=kLoop, calls=%fused_computation.57 | loop fusion | flops 2358784 | bytes 3550208 | tf_op jit(solution)/shard_map/reduce_sum | solution.py:54
  191.2 0.6 multiply_reduce_fusion.2
  191.8 0.8 fusion.40
  193.0 0.5 multiply_sqrt_fusion
  193.5 0.7 broadcast_select_fusion
  (79 shorter events, 5.6 us)
Async XLA Ops:
  7.2 104.1 %copy-start = (bf16[1152,1152]{1,0:T(8,128)(2,1)S(1)}, bf16[1152,1152]{1,0:T(8,128)(2,1)}, u32[]{:S(2)}) copy-start(bf16[1152,1152]{1,0:T(8,128)(2,1)} %param.22) | copy-start | bytes 7962628
  7.2 104.1 %all-gather.3.cloned.1.call-start = ((), (), s32[]{:S(2)}) async-start(), calls=%async_computation | async-start | bytes 7206912 | tf_op jit(solution)/shard_map/all_gather | solution.py:119
  9.3 6.1 %copy-start.10 = (bf16[16,1152]{1,0:T(8,128)(2,1)S(1)}, bf16[16,1152]{1,0:T(8,128)(2,1)}, u32[]{:S(2)}) copy-start(bf16[16,1152]{1,0:T(8,128)(2,1)} %param.20) | copy-start | bytes 110596
  9.3 140.1 %all-reduce.3.cloned.1.call-start = ((), (), s32[]{:S(2)}) async-start(), calls=%async_computation.1 | async-start | bytes 2359296 | tf_op jit(solution)/shard_map/psum | solution.py:152
  14.4 1.0 copy-start.5
  15.4 2.5 %copy-start.8 = (bf16[256,1152]{1,0:T(8,128)(2,1)S(1)}, bf16[256,1152]{1,0:T(8,128)(2,1)}, u32[]{:S(2)}) copy-start(bf16[256,1152]{1,0:T(8,128)(2,1)} %param.21) | copy-start | bytes 1769476
  15.9 1.5 copy-start.1
  15.9 95.4 %copy-start.12 = (bf16[2,1152]{1,0:T(2,128)(2,1)S(1)}, bf16[2,1152]{1,0:T(2,128)(2,1)}, u32[]{:S(2)}) copy-start(bf16[2,1152]{1,0:T(2,128)(2,1)} %param.16) | copy-start | bytes 13828
  127.6 1.3 copy-start.15
  131.2 57.0 %all-reduce.5.cloned.1.call-start = ((), (), s32[]{:S(2)}) async-start(), calls=%async_computation.2 | async-start | bytes 2359296 | tf_op jit(solution)/shard_map/psum | solution.py:152
  149.4 2.7 %copy-start.2 = (f32[2,256,1152]{2,1,0:T(8,128)S(1)}, f32[2,256,1152]{2,1,0:T(8,128)}, u32[]{:S(2)}) copy-start(f32[2,256,1152]{2,1,0:T(8,128)} %copy-done.1) | copy-start | bytes 7077892
  149.4 3.0 %copy-start.6 = (bf16[2,256,1152]{2,1,0:T(8,128)(2,1)S(1)}, bf16[2,256,1152]{2,1,0:T(8,128)(2,1)}, u32[]{:S(2)}) copy-start(bf16[2,256,1152]{2,1,0:T(8,128)(2,1)} %all-reduce.3.cloned.1.call-done) | copy-start | bytes 3538948
  152.0 1.1 copy-start.17
  153.0 1.0 copy-start.9
  153.1 1.0 copy-start.11
  153.1 1.0 copy-start.13
  154.3 2.5 %copy-start.14 = (bf16[1,1152,3,576]{1,3,2,0:T(8,128)(2,1)S(1)}, bf16[1,1152,3,576]{1,3,2,0:T(8,128)(2,1)}, u32[]{:S(2)}) copy-start(bf16[1,1152,3,576]{1,3,2,0:T(8,128)(2,1)} %param.23) | copy-start | bytes 11943940
  156.3 3.3 %copy-start.3 = (f32[2,256,1152]{2,1,0:T(8,128)}, f32[2,256,1152]{2,1,0:T(8,128)S(1)}, u32[]{:S(2)}) copy-start(f32[2,256,1152]{2,1,0:T(8,128)S(1)} %get-tuple-element.39) | copy-start | bytes 7077892
  163.6 1.3 copy-start.16
  164.9 2.2 %copy-start.18 = (s32[2]{0:T(128)S(1)}, s32[2]{0:T(128)}, u32[]{:S(2)}) copy-start(s32[2]{0:T(128)} %param.19) | copy-start | bytes 28
  188.2 2.7 %copy-start.4 = (f32[2,256,1152]{2,1,0:T(8,128)S(1)}, f32[2,256,1152]{2,1,0:T(8,128)}, u32[]{:S(2)}) copy-start(f32[2,256,1152]{2,1,0:T(8,128)} %copy-done.3) | copy-start | bytes 7077892
  188.2 3.0 %copy-start.7 = (bf16[2,256,1152]{2,1,0:T(8,128)(2,1)S(1)}, bf16[2,256,1152]{2,1,0:T(8,128)(2,1)}, u32[]{:S(2)}) copy-start(bf16[2,256,1152]{2,1,0:T(8,128)(2,1)} %all-reduce.5.cloned.1.call-done) | copy-start | bytes 3538948
Sparse Core Ops, SparseCore 0:
  10.7 100.5 all-gather.2
  131.3 18.1 all-reduce.2
  167.3 20.8 all-reduce.4
where the time goes:
time: 201 us
  waiting for transfers between devices  132 us (66%)
  matrix products  23.8 us (12%)
  other arithmetic  22.1 us (11%)
  between operations  14.1 us (7%)
  local copies, waits for them, and re-layouts  6.5 us (3%)
    all_gather x1, waiting for transfers between devices, shards(): lax.all_gather(packed, 'dp', axis=0, tiled=True)  93.2 us
    psum x2, waiting for transfers between devices, evaluate(): lax.psum(partial_value.astype(jnp.bfloat16), 'tensor').astype(jnp.float32)  38.8 us
    dot_general x2, matrix products, evaluate(): jnp.einsum('ltd,dck->ltck', attn_in, qkv_weight[0], preferred_element_typ...  8.31 us
    sub x2, other arithmetic, attend(): attn_probs = jax.nn.softmax(scores, axis=-1).astype(jnp.bfloat16)  6.48 us
    unnamed x41, local copies, waits for them, and re-layouts  5.37 us
    reduce_sum x2, other arithmetic, layer_norm(): average = jnp.mean(values, axis=-1, keepdims=True)  5.04 us
    dot_general x2, matrix products, evaluate(): jnp.einsum('ltk,dk->ltd', attended, out_weight[0], preferred_element_type...  4.45 us
    dot_general x1, matrix products, shards(): jnp.dot(cond_act, lax.all_gather(packed, 'dp', axis=0, tiled=True), prefe...  4.3 us
  transfers between devices with their start and end apart: 3, of which 3 were waited for; matrix products, arithmetic and copies ran while one was open for 3% of the time, Pallas kernels for 0%

commit v1 on v0

--- a/solution.py
+++ b/solution.py
@@ -149,7 +149,9 @@
         partial_value = jnp.einsum(
             "ltk,dk->ltd", attended, out_weight[0], preferred_element_type=jnp.float32
         )
-        attn_sum = lax.psum(partial_value.astype(jnp.bfloat16), "tensor").astype(jnp.float32)
+        attn_sum = jnp.sum(
+            lax.all_gather(partial_value.astype(jnp.bfloat16), "tensor"), axis=0
+        ).astype(jnp.float32)
         stream = stream + gate_attn[:, None] * attn_sum
         shift_final, scale_final = jnp.split(final_rows, 2, axis=1)
         final_in = modulate(stream, shift_final, scale_final)

time: 201 us -> 191 us (0.950)
  waiting for transfers between devices: 132 us -> 115 us
  other arithmetic: 22.1 us -> 28.9 us
    psum x2 -> x0, waiting for transfers between devices: 38.8 us -> none  [evaluate(): lax.psum(partial_value.astype(jnp.bfloat16), 'tensor').astype(jnp.float32)]
    all_gather x0 -> x2, waiting for transfers between devices: none -> 21.3 us  [evaluate(): lax.all_gather(partial_value.astype(jnp.bfloat16), 'tensor')]
    reduce_sum x0 -> x2, other arithmetic: none -> 6.83 us  [evaluate(): jnp.sum(lax.all_gather(partial_value.astype(jnp.bfloat16), 'tensor'), axi...]
where the time goes in v1:
time: 191 us; the launch traced here: 190 us
  waiting for transfers between devices  115 us (60%)
  other arithmetic  28.9 us (15%)
  matrix products  23.9 us (13%)
  between operations  14.1 us (7%)
  local copies, waits for them, and re-layouts  6.5 us (3%)
    all_gather x1, waiting for transfers between devices, shards(): lax.all_gather(packed, 'dp', axis=0, tiled=True)  93.2 us
    all_gather x2, waiting for transfers between devices, evaluate(): lax.all_gather(partial_value.astype(jnp.bfloat16), 'tensor')  21.3 us
    dot_general x2, matrix products, evaluate(): jnp.einsum('ltd,dck->ltck', attn_in, qkv_weight[0], preferred_element_typ...  8.31 us
    reduce_sum x2, other arithmetic, evaluate(): jnp.sum(lax.all_gather(partial_value.astype(jnp.bfloat16), 'tensor'), axi...  6.83 us
    sub x2, other arithmetic, attend(): attn_probs = jax.nn.softmax(scores, axis=-1).astype(jnp.bfloat16)  6.48 us
    unnamed x41, local copies, waits for them, and re-layouts  5.38 us
    reduce_sum x2, other arithmetic, layer_norm(): average = jnp.mean(values, axis=-1, keepdims=True)  5.04 us
    dot_general x2, matrix products, evaluate(): jnp.einsum('ltk,dk->ltd', attended, out_weight[0], preferred_element_type...  4.47 us
  transfers between devices with their start and end apart: 3, of which 3 were waited for; matrix products, arithmetic and copies ran while one was open for 3% of the time, Pallas kernels for 0%

profile of v1, /device:TPU:0, one launch (start us, length us, event | category | flops | bytes accessed | tf_op | source)
XLA Modules:
  0.0 190.1 jit_solution(5278567280981907928)
XLA Ops:
  7.2 2.1 %pad_maximum_fusion.1 = bf16[72,2880]{1,0:T(8,128)(2,1)} fusion(bf16[72,1152]{1,0:T(8,128)(2,1)} %param.26, bf16[72,1728]{1,0:T(8,128)(2,1)} %bitcast.108), kind=kLoop, calls=%fused_computation.66 | loop fusion | flops 829440 | bytes 829440 | tf_op jit(solution)/shard_map/concatenate | solution.py:111
  9.4 0.8 convert_element_type.87
  10.3 0.7 broadcast_multiply_fusion.4
  11.0 0.7 maximum_multiply_fusion
  11.8 2.4 %multiply_sine_fusion = (f32[256,576]{1,0:T(8,128)S(1)}, f32[256,576]{1,0:T(8,128)S(1)}) fusion(f32[576]{0:T(1024)S(1)} %multiply_exponential_fusion, f32[256]{0:T(256)S(1)} %iota_convert_fusion), kind=kLoop, calls=%fused_computation.55 | loop fusion | flops 147456 | bytes 1182976 | tf_op jit(solution)/shard_map/sin | solution.py:39
  14.4 1.0 copy-done.7
  15.9 1.4 copy-done.1
  18.1 93.2 %all-gather.7.cloned.1.call-done = bf16[1152,2880]{1,0:T(8,128)(2,1)} async-done(((bf16[72,2880]{1,0:T(8,128)(2,1)}), bf16[1152,2880]{1,0:T(8,128)(2,1)}) %all-gather.7.cloned.1.call-update) | async-done | bytes 6635536 | tf_op jit(solution)/shard_map/all_gather | solution.py:119
  111.3 4.3 %fusion.8 = bf16[1,2880,4]{1,2,0:T(4,128)(2,1)S(1)} fusion(bf16[1152,2880]{1,0:T(8,128)(2,1)} %all-gather.7.cloned.1.call-done, bf16[1152,1152]{1,0:T(8,128)(2,1)S(1)} %copy-done, f32[4,1152]{1,0:T(4,128)S(1)} %fusion.62, bf16[2,1152]{1,0:T(2,128)(2,1)S(1)} %copy-done.12), kind=kOutput, calls=%fused_computation.17 | convolution fusion | flops 37239552 | bytes 9335808 | tf_op jit(solution)/shard_map/dot_general | solution.py:117
  115.6 1.8 all-gather.2
  117.9 5.6 %fusion.17 = bf16[2,256,3,576]{1,3,2,0:T(8,128)(2,1)S(1)} fusion(bf16[1,1152,3,576]{1,3,2,0:T(8,128)(2,1)} %param.23, f32[2,256,1152]{2,1,0:T(8,128)} %copy-done.1, f32[2,1152]{1,0:T(2,128)S(1)} %get-tuple-element.17, f32[2,1152]{1,0:T(2,128)S(1)} %get-tuple-element.18, f32[2,256]{1,0:T(2,128)S(1)} %add_rsqrt_fusion.3, ...), kind=kOutput, calls=%fused_computation.35 | convolution fusion | flops 2042265600 | bytes 8132608 | tf_op jit(solution)/shard_map/ltd,dck->ltck/dot_general | solution.py:145
  123.5 0.8 fusion.44
  124.2 3.2 %fusion.79 = (f32[2,8,256]{2,1,0:T(8,128)S(1)}, f32[2,8,256,256]{2,3,1,0:T(8,128)S(1)}) fusion(f32[2,8,256,256]{2,3,1,0:T(8,128)S(1)} %fusion.44), kind=kOutput, calls=%fused_computation.137 | output fusion | flops 4194559 | bytes 8404992 | tf_op jit(solution)/shard_map/sub | solution.py:78
  128.0 0.8 copy-done.15
  128.8 2.2 %convolution_convert_fusion.2 = bf16[2,256,1152]{2,1,0:T(8,128)(2,1)} fusion(bf16[2,256,576]{1,2,0:T(8,128)(2,1)S(1)} %bitcast.111, bf16[1,1152,576]{1,2,0:T(8,128)(2,1)S(1)} %copy-done.15), kind=kOutput, calls=%fused_computation.19 | convolution fusion | flops 680067072 | bytes 3096576 | tf_op jit(solution)/shard_map/ltk,dk->ltd/dot_general | solution.py:149
  131.5 9.1 %all-gather.9.cloned.1.call-done = bf16[4,256,1152]{2,1,0:T(8,128)(2,1)} async-done(((bf16[2,256,1152]{2,1,0:T(8,128)(2,1)}), bf16[4,256,1152]{2,1,0:T(8,128)(2,1)}) %all-gather.9.cloned.1.call-update) | async-done | bytes 2359312 | tf_op jit(solution)/shard_map/all_gather | solution.py:153
  140.6 3.4 %reduce_sum.126 = bf16[2,256,1152]{2,1,0:T(8,128)(2,1)} reduce(bf16[2,2,256,1152]{3,2,1,0:T(8,128)(2,1)} %bitcast.101, bf16[]{:T(256)} %constant.52.clone.1), dimensions={0}, to_apply=%region_4.5 | reduce | flops 589824 | bytes 3538946 | tf_op jit(solution)/shard_map/reduce_sum | solution.py:152
  144.0 2.5 %fusion.41 = f32[2,256]{1,0:T(2,128)S(1)} fusion(f32[2,256,1152]{2,1,0:T(8,128)} %copy-done.1, bf16[2,256,1152]{2,1,0:T(8,128)(2,1)} %reduce_sum.126, f32[2,1152]{1,0:T(2,128)S(1)} %get-tuple-element.16), kind=kLoop, calls=%fused_computation.56 | loop fusion | flops 2358784 | bytes 3550208 | tf_op jit(solution)/shard_map/reduce_sum | solution.py:54
  147.0 0.6 multiply_reduce_fusion.4
  147.7 0.8 fusion.39
  148.9 2.0 %fusion.80 = (f32[2,256]{1,0:T(2,128)S(1)}, f32[2,256,1152]{2,1,0:T(8,128)S(1)}) fusion(f32[256,1152]{1,0:T(8,128)} %copy-done.7, bf16[2,256,16]{2,1,0:T(8,128)(2,1)S(1)} %convert_element_type.103, bf16[16,1152]{1,0:T(8,128)(2,1)S(1)} %copy-done.10), kind=kOutput, calls=%fused_computation.138 | convolution fusion | flops 20053504 | bytes 3594240 | tf_op jit(solution)/shard_map/ltc,cd->ltd/dot_general | solution.py:140
  151.4 2.8 %fusion.20 = bf16[2,256,3,576]{1,3,2,0:T(8,128)(2,1)S(1)} fusion(bf16[1,1152,3,576]{1,3,2,0:T(8,128)(2,1)S(1)} %copy-done.14, f32[2,256,1152]{2,1,0:T(8,128)S(1)} %get-tuple-element.39, f32[2,1152]{1,0:T(2,128)S(1)} %get-tuple-element.14, f32[2,1152]{1,0:T(2,128)S(1)} %get-tuple-element.15, f32[2,256]{1,0:T(2,128)S(1)} %add_rsqrt_fusion.1, ...), kind=kOutput, calls=%fused_computation.36 | convolution fusion | flops 2042265600 | bytes 8132608 | tf_op jit(solution)/shard_map/ltd,dck->ltck/dot_general | solution.py:145
  154.2 0.8 fusion.43
  154.9 3.2 %fusion.81 = (f32[2,8,256]{2,1,0:T(8,128)S(1)}, f32[2,8,256,256]{2,3,1,0:T(8,128)S(1)}) fusion(f32[2,8,256,256]{2,3,1,0:T(8,128)S(1)} %fusion.43), kind=kOutput, calls=%fused_computation.139 | output fusion | flops 4194559 | bytes 8404992 | tf_op jit(solution)/shard_map/sub | solution.py:78
  158.7 0.8 copy-done.16
  159.5 2.3 %convolution_convert_fusion.1 = bf16[2,256,1152]{2,1,0:T(8,128)(2,1)} fusion(bf16[2,256,576]{1,2,0:T(8,128)(2,1)S(1)} %bitcast.112, bf16[1,1152,576]{1,2,0:T(8,128)(2,1)S(1)} %copy-done.16), kind=kOutput, calls=%fused_computation.18 | convolution fusion | flops 680067072 | bytes 3096576 | tf_op jit(solution)/shard_map/ltk,dk->ltd/dot_general | solution.py:149
  161.8 12.2 %all-gather.11.cloned.1.call-done = bf16[4,256,1152]{2,1,0:T(8,128)(2,1)} async-done(((bf16[2,256,1152]{2,1,0:T(8,128)(2,1)}), bf16[4,256,1152]{2,1,0:T(8,128)(2,1)}) %all-gather.11.cloned.1.call-update) | async-done | bytes 2359312 | tf_op jit(solution)/shard_map/all_gather | solution.py:153
  174.1 3.4 %reduce_sum.132 = bf16[2,256,1152]{2,1,0:T(8,128)(2,1)} reduce(bf16[2,2,256,1152]{3,2,1,0:T(8,128)(2,1)} %bitcast.102, bf16[]{:T(256)} %constant.52.clone.1), dimensions={0}, to_apply=%region_11.12 | reduce | flops 589824 | bytes 3538946 | tf_op jit(solution)/shard_map/reduce_sum | solution.py:152
  177.5 2.5 %fusion.42 = f32[2,256]{1,0:T(2,128)S(1)} fusion(f32[2,256,1152]{2,1,0:T(8,128)} %copy-done.3, bf16[2,256,1152]{2,1,0:T(8,128)(2,1)} %reduce_sum.132, f32[2,1152]{1,0:T(2,128)S(1)} %get-tuple-element.13), kind=kLoop, calls=%fused_computation.57 | loop fusion | flops 2358784 | bytes 3550208 | tf_op jit(solution)/shard_map/reduce_sum | solution.py:54
  180.5 0.6 multiply_reduce_fusion.2
  181.1 0.8 fusion.40
  182.9 0.7 broadcast_select_fusion
  (81 shorter events, 6.7 us)
Async XLA Ops:
  7.2 104.1 %copy-start = (bf16[1152,1152]{1,0:T(8,128)(2,1)S(1)}, bf16[1152,1152]{1,0:T(8,128)(2,1)}, u32[]{:S(2)}) copy-start(bf16[1152,1152]{1,0:T(8,128)(2,1)} %param.22) | copy-start | bytes 7962628
  7.2 104.1 %all-gather.7.cloned.1.call-start = ((), (), s32[]{:S(2)}) async-start(), calls=%async_computation | async-start | bytes 7206912 | tf_op jit(solution)/shard_map/all_gather | solution.py:119
  9.3 6.1 %copy-start.10 = (bf16[16,1152]{1,0:T(8,128)(2,1)S(1)}, bf16[16,1152]{1,0:T(8,128)(2,1)}, u32[]{:S(2)}) copy-start(bf16[16,1152]{1,0:T(8,128)(2,1)} %param.20) | copy-start | bytes 110596
  9.3 131.3 %all-gather.9.cloned.1.call-start = ((), (), s32[]{:S(2)}) async-start(), calls=%async_computation.1 | async-start | bytes 3538944 | tf_op jit(solution)/shard_map/all_gather | solution.py:153
  14.4 1.0 copy-start.7
  15.4 2.5 %copy-start.8 = (bf16[256,1152]{1,0:T(8,128)(2,1)S(1)}, bf16[256,1152]{1,0:T(8,128)(2,1)}, u32[]{:S(2)}) copy-start(bf16[256,1152]{1,0:T(8,128)(2,1)} %param.21) | copy-start | bytes 1769476
  15.9 1.5 copy-start.1
  15.9 95.4 %copy-start.12 = (bf16[2,1152]{1,0:T(2,128)(2,1)S(1)}, bf16[2,1152]{1,0:T(2,128)(2,1)}, u32[]{:S(2)}) copy-start(bf16[2,1152]{1,0:T(2,128)(2,1)} %param.16) | copy-start | bytes 13828
  127.5 1.3 copy-start.15
  131.0 43.0 %all-gather.11.cloned.1.call-start = ((), (), s32[]{:S(2)}) async-start(), calls=%async_computation.2 | async-start | bytes 3538944 | tf_op jit(solution)/shard_map/all_gather | solution.py:153
  144.0 2.7 %copy-start.2 = (f32[2,256,1152]{2,1,0:T(8,128)S(1)}, f32[2,256,1152]{2,1,0:T(8,128)}, u32[]{:S(2)}) copy-start(f32[2,256,1152]{2,1,0:T(8,128)} %copy-done.1) | copy-start | bytes 7077892
  144.0 3.0 %copy-start.6 = (bf16[2,256,1152]{2,1,0:T(8,128)(2,1)S(1)}, bf16[2,256,1152]{2,1,0:T(8,128)(2,1)}, u32[]{:S(2)}) copy-start(bf16[2,256,1152]{2,1,0:T(8,128)(2,1)} %reduce_sum.126) | copy-start | bytes 3538948
  146.5 1.1 copy-start.17
  147.6 1.0 copy-start.9
  147.6 1.0 copy-start.11
  147.6 1.0 copy-start.13
  148.9 2.5 %copy-start.14 = (bf16[1,1152,3,576]{1,3,2,0:T(8,128)(2,1)S(1)}, bf16[1,1152,3,576]{1,3,2,0:T(8,128)(2,1)}, u32[]{:S(2)}) copy-start(bf16[1,1152,3,576]{1,3,2,0:T(8,128)(2,1)} %param.23) | copy-start | bytes 11943940
  150.9 3.3 %copy-start.3 = (f32[2,256,1152]{2,1,0:T(8,128)}, f32[2,256,1152]{2,1,0:T(8,128)S(1)}, u32[]{:S(2)}) copy-start(f32[2,256,1152]{2,1,0:T(8,128)S(1)} %get-tuple-element.39) | copy-start | bytes 7077892
  158.2 1.3 copy-start.16
  159.5 2.3 %copy-start.18 = (s32[2]{0:T(128)S(1)}, s32[2]{0:T(128)}, u32[]{:S(2)}) copy-start(s32[2]{0:T(128)} %param.19) | copy-start | bytes 28
  177.5 2.7 %copy-start.4 = (f32[2,256,1152]{2,1,0:T(8,128)S(1)}, f32[2,256,1152]{2,1,0:T(8,128)}, u32[]{:S(2)}) copy-start(f32[2,256,1152]{2,1,0:T(8,128)} %copy-done.3) | copy-start | bytes 7077892
  177.5 3.0 %copy-start.5 = (bf16[2,256,1152]{2,1,0:T(8,128)(2,1)S(1)}, bf16[2,256,1152]{2,1,0:T(8,128)(2,1)}, u32[]{:S(2)}) copy-start(bf16[2,256,1152]{2,1,0:T(8,128)(2,1)} %reduce_sum.132) | copy-start | bytes 3538948
Sparse Core Ops, SparseCore 0:
  10.7 100.5 all-gather.6
  131.2 9.3 all-gather.8
  161.9 12.1 all-gather.10
